TPU v7x, 32 devices: a whole 2x2x4 slice. The times are simulated.
32 devices in a mesh: gx: 4 (over z), gy: 2 (over core), gz: 4 (over y, x).
Axes of the slice: x: 2, y: 2, z: 4, core: 2. Of those that a mesh axis runs over, the one named last changes fastest.
Arguments:
- e_field: float32 [3, 16, 32, 512], P(None, 'gx', 'gy', 'gz'), may hold values from -6 to 6
- h_field: float32 [3, 16, 32, 512], P(None, 'gx', 'gy', 'gz'), may hold values from -6 to 6
- current: float32 [3, 16, 32, 512], P(None, 'gx', 'gy', 'gz'), may hold values from -6 to 6
- material: int32 [16, 32, 512], P('gx', 'gy', 'gz'), may hold values from 0 to 2
- sigma_table: float32 [3], replicated, may hold values from 0.05 to 2
- gamma_table: float32 [3], replicated, may hold values from 0.05 to 1
- plasma_table: float32 [3], replicated, may hold values from 0.3 to 2
- g_kernel: float32 [4], replicated, may hold values from -4 to 4
- surf_cell: int32 [4, 2, 4, 1024], P('gx', 'gy', 'gz'), may hold values from 0 to 8191
- surf_owner: int32 [4, 2, 4, 1024, 1], P('gx', 'gy', 'gz'), may hold values from 0 to 7; in each aligned block of 1024 rows (0 to 1023, 1024 to 2047, ..., all dimensions but the last counted through in order) at most 192 rows name the same one
- surf_tile: int32 [4, 2, 4, 1024], P('gx', 'gy', 'gz'), may hold values from 0 to 127
- surf_normal: int32 [4, 2, 4, 1024], P('gx', 'gy', 'gz'), may hold values from 0 to 5
- row_count: int32 [4, 2, 4], P('gx', 'gy', 'gz'), may hold values from 256 to 1024, as said below
Outputs:
- e_out: float32 [3, 16, 32, 512], P(None, 'gx', 'gy', 'gz')
- h_out: float32 [3, 16, 32, 512], P(None, 'gx', 'gy', 'gz')
- force: float32 [3, 4096], P(None, ('gx', 'gy', 'gz'))
Inputs may be any that keep to these rules, and one draw needn't show every extreme that they name: `surf_owner`: among the slots of one device no owner is named more than 192 times, a bound that some block reaches. `row_count`: some brick has all 1024 slots live.
All inputs are finite; a program needn't handle non-finite values.
Results may differ from a plain program's by a relative error of at most 0.00019.
Values sent between devices are 32-bit elements; how exact they have to be, the bound alone decides.
No kernel may reach another device: no remote copies, remote signals or barrier semaphores. Data moves between devices by JAX's collectives and lax.ppermute only.
A program may use at most 64 MiB of HBM per device.

v0:
```python
import jax
import jax.numpy as jnp
from jax import lax
from jax.sharding import PartitionSpec as P

TILE_DEV = 128
STEP_DT = 0.5
FACE_AREA = 0.25


def passed_along(shard, axis, by):
    peers = lax.axis_size(axis)
    pairs = [(i, i + by) for i in range(peers) if 0 <= i + by < peers]
    return lax.ppermute(shard, axis, pairs)


def lookup(material, table):
    result = jnp.zeros(material.shape, table.dtype)
    for which in range(table.shape[0]):
        result = result + jnp.where(material == which, table[which], jnp.zeros((), table.dtype))
    return result


def coefficients(material, sigma_table, gamma_table, plasma_table):
    sigma = lookup(material, sigma_table)
    gamma = lookup(material, gamma_table)
    plasma = lookup(material, plasma_table)
    keep_e = (1.0 - sigma * STEP_DT / 2) / (1.0 + sigma * STEP_DT / 2)
    gain_e = STEP_DT / (1.0 + sigma * STEP_DT / 2)
    keep_j = (1.0 - gamma * STEP_DT / 2) / (1.0 + gamma * STEP_DT / 2)
    gain_j = plasma * STEP_DT / (1.0 + gamma * STEP_DT / 2)
    return (keep_e, gain_e, keep_j, gain_j)


def row_forces(elec_rows, magn_rows, normal):
    axis_of = normal // 2
    sign_of = (1 - 2 * (normal % 2)).astype(elec_rows.dtype)
    picked = (axis_of[None, :] == jnp.arange(3, dtype=jnp.int32)[:, None]).astype(elec_rows.dtype)
    elec_n = jnp.sum(elec_rows * picked, axis=0)
    magn_n = jnp.sum(magn_rows * picked, axis=0)
    energy = 0.5 * (jnp.sum(elec_rows * elec_rows, axis=0) + jnp.sum(magn_rows * magn_rows, axis=0))
    return sign_of * (elec_rows * elec_n + magn_rows * magn_n - picked * energy)


def curl_upper(electric):
    rim_x = passed_along(electric[1:3, :1], "gx", -1)
    rim_y = passed_along(electric[0::2, :, :1], "gy", -1)
    rim_z = passed_along(electric[0:2, :, :, :1], "gz", -1)
    elec_x, elec_y, elec_z = (electric[0], electric[1], electric[2])
    y_next_x = jnp.concatenate([elec_y[1:], rim_x[0]], 0)
    z_next_x = jnp.concatenate([elec_z[1:], rim_x[1]], 0)
    x_next_y = jnp.concatenate([elec_x[:, 1:], rim_y[0]], 1)
    z_next_y = jnp.concatenate([elec_z[:, 1:], rim_y[1]], 1)
    x_next_z = jnp.concatenate([elec_x[:, :, 1:], rim_z[0]], 2)
    y_next_z = jnp.concatenate([elec_y[:, :, 1:], rim_z[1]], 2)
    curl_x = z_next_y - elec_z - (y_next_z - elec_y)
    curl_y = x_next_z - elec_x - (z_next_x - elec_z)
    curl_z = y_next_x - elec_y - (x_next_y - elec_x)
    return jnp.stack([curl_x, curl_y, curl_z])


def curl_lower(magnetic):
    rim_x = passed_along(magnetic[1:3, -1:], "gx", 1)
    rim_y = passed_along(magnetic[0::2, :, -1:], "gy", 1)
    rim_z = passed_along(magnetic[0:2, :, :, -1:], "gz", 1)
    magn_x, magn_y, magn_z = (magnetic[0], magnetic[1], magnetic[2])
    y_prev_x = jnp.concatenate([rim_x[0], magn_y[:-1]], 0)
    z_prev_x = jnp.concatenate([rim_x[1], magn_z[:-1]], 0)
    x_prev_y = jnp.concatenate([rim_y[0], magn_x[:, :-1]], 1)
    z_prev_y = jnp.concatenate([rim_y[1], magn_z[:, :-1]], 1)
    x_prev_z = jnp.concatenate([rim_z[0], magn_x[:, :, :-1]], 2)
    y_prev_z = jnp.concatenate([rim_z[1], magn_y[:, :, :-1]], 2)
    curl_x = magn_z - z_prev_y - (magn_y - y_prev_z)
    curl_y = magn_x - x_prev_z - (magn_z - z_prev_x)
    curl_z = magn_y - y_prev_x - (magn_x - x_prev_y)
    return jnp.stack([curl_x, curl_y, curl_z])


def local(
    e_field,
    h_field,
    current,
    material,
    sigma_table,
    gamma_table,
    plasma_table,
    g_kernel,
    surf_cell,
    surf_owner,
    surf_tile,
    surf_normal,
    row_count,
):
    keep_e, gain_e, keep_j, gain_j = coefficients(material, sigma_table, gamma_table, plasma_table)
    electric, magnetic, drude = (e_field, h_field, current)
    slot_cells = surf_cell.reshape(-1)
    normal = surf_normal.reshape(-1)
    owners = surf_owner.reshape(-1)
    tile_ids = surf_tile.reshape(-1)
    slot_total = slot_cells.shape[0]
    live_mask = (jnp.arange(slot_total, dtype=jnp.int32) < row_count.reshape(())).astype(
        jnp.float32
    )
    summed = jnp.zeros((3, slot_total), jnp.float32)
    for moment in range(g_kernel.shape[0]):
        magnetic = magnetic - STEP_DT * curl_upper(electric)
        curl_magn = curl_lower(magnetic)
        drude = keep_j * drude + gain_j * electric
        electric = keep_e * electric + gain_e * (curl_magn - drude)
        elec_rows = electric.reshape(3, -1)[:, slot_cells]
        magn_rows = magnetic.reshape(3, -1)[:, slot_cells]
        summed = summed + g_kernel[moment] * row_forces(elec_rows, magn_rows, normal)
    row_force = FACE_AREA * summed * live_mask
    groups = lax.axis_size("gx") * lax.axis_size("gy")
    capacity = 3 * slot_total // (2 * groups)
    owner_hot = (owners[:, None] == jnp.arange(groups, dtype=jnp.int32)[None, :]).astype(jnp.int32)
    ranks = jnp.sum(jnp.cumsum(owner_hot, axis=0) * owner_hot, axis=1) - 1
    force_buf = jnp.zeros((3, capacity, groups), jnp.float32).at[:, ranks, owners].set(row_force)
    tile_buf = (
        jnp.full((1, capacity, groups), -1.0, jnp.float32)
        .at[0, ranks, owners]
        .set(tile_ids.astype(jnp.float32))
    )
    got_force, got_tile = (
        lax.all_to_all(force_buf, ("gx", "gy"), split_axis=2, concat_axis=2, tiled=True),
        lax.all_to_all(tile_buf, ("gx", "gy"), split_axis=2, concat_axis=2, tiled=True),
    )
    tile_hot = (
        got_tile[0][:, :, None] == jnp.arange(TILE_DEV, dtype=jnp.float32)[None, None, :]
    ).astype(jnp.float32)
    force = jnp.einsum("acs,cst->at", got_force, tile_hot, precision=lax.Precision.HIGHEST)
    return (electric, magnetic, force)


def solution(mesh):
    return jax.shard_map(
        local,
        mesh=mesh,
        in_specs=(
            P(None, "gx", "gy", "gz"),
            P(None, "gx", "gy", "gz"),
            P(None, "gx", "gy", "gz"),
            P("gx", "gy", "gz"),
            P(),
            P(),
            P(),
            P(),
            P("gx", "gy", "gz", None),
            P("gx", "gy", "gz", None, None),
            P("gx", "gy", "gz", None),
            P("gx", "gy", "gz", None),
            P("gx", "gy", "gz"),
        ),
        out_specs=(
            P(None, "gx", "gy", "gz"),
            P(None, "gx", "gy", "gz"),
            P(None, ("gx", "gy", "gz")),
        ),
        check_vma=False,
    )
```

profile of v0, /device:TPU:0, one launch (start us, length us, event | category | flops | bytes accessed | tf_op | source)
XLA Modules:
  0.0 190.6 jit_solution(9184814041773252684)
XLA Ops:
  11.8 4.3 %scatter_custom_fusion.1 = f32[1536]{0:T(1024)S(1)} fusion(s32[1024]{0:T(1024)S(1)} %broadcast_select_fusion, f32[1024]{0:T(1024)S(1)} %bitcast.311, f32[]{:T(128)} %constant.91.clone.1), kind=kCustom, calls=%fused_computation.263 | custom fusion | bytes 6148
  16.8 7.9 %all-to-all-start.1 = ((f32[1,192,8]{1,0,2:T(1,128)}), f32[1,192,8]{1,0,2:T(1,128)S(1)}, u32[]{:S(2)}, u32[]{:S(2)}) async-start(f32[1,192,8]{1,0,2:T(1,128)} %bitcast.99), calls=%async_computation.1 | async-start | bytes 16384 | tf_op jit(solution)/shard_map/all_to_all | solution.py:126
  37.7 2.7 %subtract_divide_fusion.1 = (f32[4,16,128]{2,1,0:T(8,128)S(1)}, pred[4,16,128]{2,1,0:T(8,128)(4,1)S(1)}, pred[4,16,128]{2,1,0:T(8,128)(4,1)S(1)}, pred[4,16,128]{2,1,0:T(8,128)(4,1)S(1)}) fusion(f32[]{:T(128)} %bitcast.2, f32[]{:T(128)} %bitcast.1, f32[]{:T(128)} %bitcast, s32[4,16,128]{2,1,0:T(8,128)} %param.16), kind=kLoop, calls=%fused_computation.152 | loop fusion | flops 98304 | bytes 90124 | tf_op jit(solution)/shard_map/div | solution.py:28
  40.4 5.7 %add_divide_fusion = (f32[4,16,128]{2,1,0:T(8,128)S(1)}, f32[4,16,128]{2,1,0:T(8,128)S(1)}, f32[4,16,128]{2,1,0:T(8,128)S(1)}) fusion(pred[4,16,128]{2,1,0:T(8,128)(4,1)S(1)} %get-tuple-element.38, pred[4,16,128]{2,1,0:T(8,128)(4,1)S(1)} %get-tuple-element.37, pred[4,16,128]{2,1,0:T(8,128)(4,1)S(1)} %get-tuple-element.36, f32[]{:T(128)} %bitcast.2, ...), kind=kLoop, calls=%fused_computation.155 | loop fusion | flops 196608 | bytes 122916 | tf_op jit(solution)/shard_map/div | solution.py:29
  50.6 3.5 %collective-permute-start.5 = (f32[2,1,16,128]{3,2,1,0:T(8,128)S(1)}, f32[2,1,16,128]{3,2,1,0:T(8,128)S(1)}, u32[]{:S(2)}, u32[]{:S(2)}) collective-permute-start(f32[2,1,16,128]{3,2,1,0:T(8,128)S(1)} %slice.704), channel_id=1, source_target_pairs={{0,8},{8,16},{16,24},{1,9},{9,17},{17,25},{2,10},{10,18},{18,26},{... | collective-permute-start | bytes 49160 | tf_op jit(solution)/shard_map/ppermute | solution.py:14
  54.2 4.3 %collective-permute-start.4 = (f32[2,4,16,1]{3,2,1,0:T(8,128)S(1)}, f32[2,4,16,1]{3,2,1,0:T(8,128)S(1)}, u32[]{:S(2)}, u32[]{:S(2)}) collective-permute-start(f32[2,4,16,1]{3,2,1,0:T(8,128)S(1)} %slice.698), channel_id=1, source_target_pairs={{0,1},{1,2},{2,3},{4,5},{5,6},{6,7},{8,9},{9,10},{10,11},{12,13},{... | collective-permute-start | bytes 1544 | tf_op jit(solution)/shard_map/ppermute | solution.py:14
  58.5 2.6 %copy.46 = f32[3,4,16,128]{0,3,2,1:T(8,128)} copy(f32[3,4,16,128]{3,2,1,0:T(8,128)S(1)} %fusion.3) | data formatting | bytes 196608 | tf_op jit(solution)/shard_map/sub | solution.py:106
  61.1 5.0 %gather_fusion.1 = f32[1024,3]{1,0:T(8,128)S(1)} fusion(f32[3,8192]{0,1:T(8,128)} %bitcast.295, s32[1024]{0:T(1024)S(1)} %broadcast_clamp_fusion), kind=kCustom, calls=%fused_computation.1 | custom fusion | bytes 28672 | tf_op jit(solution)/shard_map/gather | solution.py:111
  70.7 2.6 %copy.44 = f32[3,4,16,128]{0,3,2,1:T(8,128)} copy(f32[3,4,16,128]{3,2,1,0:T(8,128)S(1)} %fusion.5) | data formatting | bytes 196608 | tf_op jit(solution)/shard_map/add | solution.py:109
  73.3 5.0 %gather_fusion = f32[1024,3]{1,0:T(8,128)S(1)} fusion(f32[3,8192]{0,1:T(8,128)} %bitcast.296, s32[1024]{0:T(1024)S(1)} %broadcast_clamp_fusion), kind=kCustom, calls=%fused_computation | custom fusion | bytes 28672 | tf_op jit(solution)/shard_map/gather | solution.py:110
  78.9 3.0 %collective-permute-start.9 = (f32[2,4,1,128]{3,2,1,0:T(1,128)S(1)}, f32[2,4,1,128]{3,2,1,0:T(1,128)S(1)}, u32[]{:S(2)}, u32[]{:S(2)}) collective-permute-start(f32[2,4,1,128]{3,2,1,0:T(1,128)S(1)} %slice.573), channel_id=1, source_target_pairs={{0,4},{1,5},{2,6},{3,7},{8,12},{9,13},{10,14},{11,15},{16,20},{17,... | collective-permute-start | bytes 12296 | tf_op jit(solution)/shard_map/ppermute | solution.py:14
  81.9 4.3 %collective-permute-start.11 = (f32[2,1,16,128]{3,2,1,0:T(8,128)S(1)}, f32[2,1,16,128]{3,2,1,0:T(8,128)S(1)}, u32[]{:S(2)}, u32[]{:S(2)}) collective-permute-start(f32[2,1,16,128]{3,2,1,0:T(8,128)S(1)} %slice.738), channel_id=1, source_target_pairs={{0,8},{8,16},{16,24},{1,9},{9,17},{17,25},{2,10},{10,18},{18,26},{... | collective-permute-start | bytes 49160 | tf_op jit(solution)/shard_map/ppermute | solution.py:14
  86.2 4.9 %collective-permute-start.10 = (f32[2,4,16,1]{3,2,1,0:T(8,128)S(1)}, f32[2,4,16,1]{3,2,1,0:T(8,128)S(1)}, u32[]{:S(2)}, u32[]{:S(2)}) collective-permute-start(f32[2,4,16,1]{3,2,1,0:T(8,128)S(1)} %slice.732), channel_id=1, source_target_pairs={{0,1},{1,2},{2,3},{4,5},{5,6},{6,7},{8,9},{9,10},{10,11},{12,13},{... | collective-permute-start | bytes 1544 | tf_op jit(solution)/shard_map/ppermute | solution.py:14
  91.1 2.6 %copy.50 = f32[3,4,16,128]{0,3,2,1:T(8,128)} copy(f32[3,4,16,128]{3,2,1,0:T(8,128)S(1)} %fusion.6) | data formatting | bytes 196608 | tf_op jit(solution)/shard_map/sub | solution.py:106
  93.8 5.0 %gather_fusion.3 = f32[1024,3]{1,0:T(8,128)S(1)} fusion(f32[3,8192]{0,1:T(8,128)} %bitcast.297, s32[1024]{0:T(1024)S(1)} %broadcast_clamp_fusion), kind=kCustom, calls=%fused_computation.3 | custom fusion | bytes 28672 | tf_op jit(solution)/shard_map/gather | solution.py:111
  106.0 5.0 %gather_fusion.2 = f32[1024,3]{1,0:T(8,128)S(1)} fusion(f32[3,8192]{0,1:T(8,128)} %bitcast.298, s32[1024]{0:T(1024)S(1)} %broadcast_clamp_fusion), kind=kCustom, calls=%fused_computation.2 | custom fusion | bytes 28672 | tf_op jit(solution)/shard_map/gather | solution.py:110
  111.5 3.0 %collective-permute-start.15 = (f32[2,4,1,128]{3,2,1,0:T(1,128)S(1)}, f32[2,4,1,128]{3,2,1,0:T(1,128)S(1)}, u32[]{:S(2)}, u32[]{:S(2)}) collective-permute-start(f32[2,4,1,128]{3,2,1,0:T(1,128)S(1)} %slice.609), channel_id=1, source_target_pairs={{0,4},{1,5},{2,6},{3,7},{8,12},{9,13},{10,14},{11,15},{16,20},{17,... | collective-permute-start | bytes 12296 | tf_op jit(solution)/shard_map/ppermute | solution.py:14
  114.5 4.3 %collective-permute-start.17 = (f32[2,1,16,128]{3,2,1,0:T(8,128)S(1)}, f32[2,1,16,128]{3,2,1,0:T(8,128)S(1)}, u32[]{:S(2)}, u32[]{:S(2)}) collective-permute-start(f32[2,1,16,128]{3,2,1,0:T(8,128)S(1)} %slice.772), channel_id=1, source_target_pairs={{0,8},{8,16},{16,24},{1,9},{9,17},{17,25},{2,10},{10,18},{18,26},{... | collective-permute-start | bytes 49160 | tf_op jit(solution)/shard_map/ppermute | solution.py:14
  118.8 5.2 %collective-permute-start.16 = (f32[2,4,16,1]{3,2,1,0:T(8,128)S(1)}, f32[2,4,16,1]{3,2,1,0:T(8,128)S(1)}, u32[]{:S(2)}, u32[]{:S(2)}) collective-permute-start(f32[2,4,16,1]{3,2,1,0:T(8,128)S(1)} %slice.766), channel_id=1, source_target_pairs={{0,1},{1,2},{2,3},{4,5},{5,6},{6,7},{8,9},{9,10},{10,11},{12,13},{... | collective-permute-start | bytes 1544 | tf_op jit(solution)/shard_map/ppermute | solution.py:14
  124.0 2.6 %copy.54 = f32[3,4,16,128]{0,3,2,1:T(8,128)} copy(f32[3,4,16,128]{3,2,1,0:T(8,128)S(1)} %fusion.9) | data formatting | bytes 196608 | tf_op jit(solution)/shard_map/sub | solution.py:106
  126.6 5.0 %gather_fusion.5 = f32[1024,3]{1,0:T(8,128)S(1)} fusion(f32[3,8192]{0,1:T(8,128)} %bitcast.299, s32[1024]{0:T(1024)S(1)} %broadcast_clamp_fusion), kind=kCustom, calls=%fused_computation.5 | custom fusion | bytes 28672 | tf_op jit(solution)/shard_map/gather | solution.py:111
  136.2 2.6 %copy.52 = f32[3,4,16,128]{0,3,2,1:T(8,128)} copy(f32[3,4,16,128]{3,2,1,0:T(8,128)S(1)} %fusion.11) | data formatting | bytes 196608 | tf_op jit(solution)/shard_map/add | solution.py:109
  138.8 5.0 %gather_fusion.4 = f32[1024,3]{1,0:T(8,128)S(1)} fusion(f32[3,8192]{0,1:T(8,128)} %bitcast.300, s32[1024]{0:T(1024)S(1)} %broadcast_clamp_fusion), kind=kCustom, calls=%fused_computation.4 | custom fusion | bytes 28672 | tf_op jit(solution)/shard_map/gather | solution.py:110
  144.4 3.0 %collective-permute-start.21 = (f32[2,4,1,128]{3,2,1,0:T(1,128)S(1)}, f32[2,4,1,128]{3,2,1,0:T(1,128)S(1)}, u32[]{:S(2)}, u32[]{:S(2)}) collective-permute-start(f32[2,4,1,128]{3,2,1,0:T(1,128)S(1)} %slice.645), channel_id=1, source_target_pairs={{0,4},{1,5},{2,6},{3,7},{8,12},{9,13},{10,14},{11,15},{16,20},{17,... | collective-permute-start | bytes 12296 | tf_op jit(solution)/shard_map/ppermute | solution.py:14
  147.4 4.3 %collective-permute-start.23 = (f32[2,1,16,128]{3,2,1,0:T(8,128)S(1)}, f32[2,1,16,128]{3,2,1,0:T(8,128)S(1)}, u32[]{:S(2)}, u32[]{:S(2)}) collective-permute-start(f32[2,1,16,128]{3,2,1,0:T(8,128)S(1)} %slice.806), channel_id=1, source_target_pairs={{0,8},{8,16},{16,24},{1,9},{9,17},{17,25},{2,10},{10,18},{18,26},{... | collective-permute-start | bytes 49160 | tf_op jit(solution)/shard_map/ppermute | solution.py:14
  151.7 5.2 %collective-permute-start.22 = (f32[2,4,16,1]{3,2,1,0:T(8,128)S(1)}, f32[2,4,16,1]{3,2,1,0:T(8,128)S(1)}, u32[]{:S(2)}, u32[]{:S(2)}) collective-permute-start(f32[2,4,16,1]{3,2,1,0:T(8,128)S(1)} %slice.800), channel_id=1, source_target_pairs={{0,1},{1,2},{2,3},{4,5},{5,6},{6,7},{8,9},{9,10},{10,11},{12,13},{... | collective-permute-start | bytes 1544 | tf_op jit(solution)/shard_map/ppermute | solution.py:14
  159.5 5.0 %gather_fusion.7 = f32[1024,3]{1,0:T(8,128)S(1)} fusion(f32[3,8192]{0,1:T(8,128)} %bitcast.301, s32[1024]{0:T(1024)S(1)} %broadcast_clamp_fusion), kind=kCustom, calls=%fused_computation.7 | custom fusion | bytes 28672 | tf_op jit(solution)/shard_map/gather | solution.py:111
  167.6 5.0 %gather_fusion.6 = f32[1024,3]{1,0:T(8,128)S(1)} fusion(f32[3,8192]{0,1:T(8,128)} %bitcast.294, s32[1024]{0:T(1024)S(1)} %broadcast_clamp_fusion), kind=kCustom, calls=%fused_computation.6 | custom fusion | bytes 28672 | tf_op jit(solution)/shard_map/gather | solution.py:110
  173.0 2.7 %fusion.50 = f32[1024,3]{0,1:T(4,128)S(1)} fusion(f32[1024,3]{0,1:T(4,128)S(1)} %copy.59, f32[1024,3]{0,1:T(4,128)S(1)} %copy.57, f32[1024,3]{0,1:T(4,128)S(1)} %copy.55, f32[1024,3]{0,1:T(4,128)S(1)} %copy.53, f32[1024,3]{0,1:T(4,128)S(1)} %copy.51, f32[1024,3]{0,1:T(4,128)S(1)} %copy.49, f32[1024,3]{0,1:T(4,128)S(1)} %copy.47, f32[1024,3]{0,1:T(4,128)S(1)} %copy.45, ...), kind=kLoop, calls=%fused_computation.195 | loop fusion | flops 101376 | bytes 172048 | tf_op jit(solution)/shard_map/mul | solution.py:113
  175.9 3.3 %scatter_custom_fusion = f32[3,1536]{0,1:T(8,128)S(1)} fusion(s32[1024]{0:T(1024)S(1)} %broadcast_select_fusion.1, f32[1024,3]{1,0:T(8,128)S(1)} %copy.60, f32[]{:T(128)} %constant.82.clone.1), kind=kCustom, calls=%fused_computation.12 | custom fusion | bytes 18436
  180.2 3.6 %all-to-all-start = ((f32[3,192,8]{1,0,2:T(4,128)}), f32[3,192,8]{1,0,2:T(4,128)S(1)}, u32[]{:S(2)}, u32[]{:S(2)}) async-start(f32[3,192,8]{1,0,2:T(4,128)} %bitcast.97), calls=%async_computation | async-start | bytes 65536 | tf_op jit(solution)/shard_map/all_to_all | solution.py:125
  183.8 5.7 %all-to-all-done = f32[3,192,8]{1,0,2:T(4,128)S(1)} async-done(((f32[3,192,8]{1,0,2:T(4,128)}), f32[3,192,8]{1,0,2:T(4,128)S(1)}, u32[]{:S(2)}, u32[]{:S(2)}) %all-to-all-start) | async-done | bytes 18464 | tf_op jit(solution)/shard_map/all_to_all | solution.py:125
  (203 shorter events, 54.0 us)
Async XLA Ops:
  1.4 44.8 %collective-permute-start = (f32[2,4,1,128]{3,2,1,0:T(1,128)S(1)}, f32[2,4,1,128]{3,2,1,0:T(1,128)S(1)}, u32[]{:S(2)}, u32[]{:S(2)}) collective-permute-start(f32[2,4,1,128]{3,2,1,0:T(1,128)S(1)} %slice.514), channel_id=1, source_target_pairs={{4,0},{5,1},{6,2},{7,3},{12,8},{13,9},{14,10},{15,11},{20,16},{21,... | collective-permute-start | bytes 12296 | tf_op jit(solution)/shard_map/ppermute | solution.py:14
  3.4 42.8 %collective-permute-start.2 = (f32[2,1,16,128]{3,2,1,0:T(8,128)S(1)}, f32[2,1,16,128]{3,2,1,0:T(8,128)S(1)}, u32[]{:S(2)}, u32[]{:S(2)}) collective-permute-start(f32[2,1,16,128]{3,2,1,0:T(8,128)S(1)} %slice.524), channel_id=1, source_target_pairs={{8,0},{16,8},{24,16},{9,1},{17,9},{25,17},{10,2},{18,10},{26,18},{... | collective-permute-start | bytes 49160 | tf_op jit(solution)/shard_map/ppermute | solution.py:14
  16.8 163.3 %all-to-all-start.1 = ((f32[1,192,8]{1,0,2:T(1,128)}), f32[1,192,8]{1,0,2:T(1,128)S(1)}, u32[]{:S(2)}, u32[]{:S(2)}) async-start(f32[1,192,8]{1,0,2:T(1,128)} %bitcast.99), calls=%async_computation.1 | async-start | bytes 16384 | tf_op jit(solution)/shard_map/all_to_all | solution.py:126
  24.7 41.8 %copy-start = (f32[3,4,16,128]{3,2,1,0:T(8,128)S(1)}, f32[3,4,16,128]{3,2,1,0:T(8,128)}, u32[]{:S(2)}) copy-start(f32[3,4,16,128]{3,2,1,0:T(8,128)} %param.13) | copy-start | bytes 294916
  24.7 41.8 %copy-start.3 = (f32[3,4,16,128]{3,2,1,0:T(8,128)S(1)}, f32[3,4,16,128]{3,2,1,0:T(8,128)}, u32[]{:S(2)}) copy-start(f32[3,4,16,128]{3,2,1,0:T(8,128)} %param.15) | copy-start | bytes 294916
  25.6 20.6 %collective-permute-start.1 = (f32[2,4,16,1]{3,2,1,0:T(8,128)S(1)}, f32[2,4,16,1]{3,2,1,0:T(8,128)S(1)}, u32[]{:S(2)}, u32[]{:S(2)}) collective-permute-start(f32[2,4,16,1]{3,2,1,0:T(8,128)S(1)} %slice.518), channel_id=1, source_target_pairs={{1,0},{2,1},{3,2},{5,4},{6,5},{7,6},{9,8},{10,9},{11,10},{13,12},{... | collective-permute-start | bytes 1544 | tf_op jit(solution)/shard_map/ppermute | solution.py:14
  48.2 18.1 %collective-permute-start.3 = (f32[2,4,1,128]{3,2,1,0:T(1,128)S(1)}, f32[2,4,1,128]{3,2,1,0:T(1,128)S(1)}, u32[]{:S(2)}, u32[]{:S(2)}) collective-permute-start(f32[2,4,1,128]{3,2,1,0:T(1,128)S(1)} %slice.531), channel_id=1, source_target_pairs={{0,4},{1,5},{2,6},{3,7},{8,12},{9,13},{10,14},{11,15},{16,20},{17,... | collective-permute-start | bytes 12296 | tf_op jit(solution)/shard_map/ppermute | solution.py:14
  50.6 15.7 %collective-permute-start.5 = (f32[2,1,16,128]{3,2,1,0:T(8,128)S(1)}, f32[2,1,16,128]{3,2,1,0:T(8,128)S(1)}, u32[]{:S(2)}, u32[]{:S(2)}) collective-permute-start(f32[2,1,16,128]{3,2,1,0:T(8,128)S(1)} %slice.704), channel_id=1, source_target_pairs={{0,8},{8,16},{16,24},{1,9},{9,17},{17,25},{2,10},{10,18},{18,26},{... | collective-permute-start | bytes 49160 | tf_op jit(solution)/shard_map/ppermute | solution.py:14
  54.2 12.2 %collective-permute-start.4 = (f32[2,4,16,1]{3,2,1,0:T(8,128)S(1)}, f32[2,4,16,1]{3,2,1,0:T(8,128)S(1)}, u32[]{:S(2)}, u32[]{:S(2)}) collective-permute-start(f32[2,4,16,1]{3,2,1,0:T(8,128)S(1)} %slice.698), channel_id=1, source_target_pairs={{0,1},{1,2},{2,3},{4,5},{5,6},{6,7},{8,9},{9,10},{10,11},{12,13},{... | collective-permute-start | bytes 1544 | tf_op jit(solution)/shard_map/ppermute | solution.py:14
  61.1 17.6 %copy-start.2 = (f32[3,4,16,128]{3,2,1,0:T(8,128)S(1)}, f32[3,4,16,128]{3,2,1,0:T(8,128)}, u32[]{:S(2)}) copy-start(f32[3,4,16,128]{3,2,1,0:T(8,128)} %param.14) | copy-start | bytes 294916
  66.7 11.8 %collective-permute-start.6 = (f32[2,4,1,128]{3,2,1,0:T(1,128)S(1)}, f32[2,4,1,128]{3,2,1,0:T(1,128)S(1)}, u32[]{:S(2)}, u32[]{:S(2)}) collective-permute-start(f32[2,4,1,128]{3,2,1,0:T(1,128)S(1)} %slice.556), channel_id=1, source_target_pairs={{4,0},{5,1},{6,2},{7,3},{12,8},{13,9},{14,10},{15,11},{20,16},{21,... | collective-permute-start | bytes 12296 | tf_op jit(solution)/shard_map/ppermute | solution.py:14
  68.0 10.6 %collective-permute-start.8 = (f32[2,1,16,128]{3,2,1,0:T(8,128)S(1)}, f32[2,1,16,128]{3,2,1,0:T(8,128)S(1)}, u32[]{:S(2)}, u32[]{:S(2)}) collective-permute-start(f32[2,1,16,128]{3,2,1,0:T(8,128)S(1)} %slice.722), channel_id=1, source_target_pairs={{8,0},{16,8},{24,16},{9,1},{17,9},{25,17},{10,2},{18,10},{26,18},{... | collective-permute-start | bytes 49160 | tf_op jit(solution)/shard_map/ppermute | solution.py:14
  69.3 9.2 %collective-permute-start.7 = (f32[2,4,16,1]{3,2,1,0:T(8,128)S(1)}, f32[2,4,16,1]{3,2,1,0:T(8,128)S(1)}, u32[]{:S(2)}, u32[]{:S(2)}) collective-permute-start(f32[2,4,16,1]{3,2,1,0:T(8,128)S(1)} %slice.716), channel_id=1, source_target_pairs={{1,0},{2,1},{3,2},{5,4},{6,5},{7,6},{9,8},{10,9},{11,10},{13,12},{... | collective-permute-start | bytes 1544 | tf_op jit(solution)/shard_map/ppermute | solution.py:14
  78.9 20.1 %collective-permute-start.9 = (f32[2,4,1,128]{3,2,1,0:T(1,128)S(1)}, f32[2,4,1,128]{3,2,1,0:T(1,128)S(1)}, u32[]{:S(2)}, u32[]{:S(2)}) collective-permute-start(f32[2,4,1,128]{3,2,1,0:T(1,128)S(1)} %slice.573), channel_id=1, source_target_pairs={{0,4},{1,5},{2,6},{3,7},{8,12},{9,13},{10,14},{11,15},{16,20},{17,... | collective-permute-start | bytes 12296 | tf_op jit(solution)/shard_map/ppermute | solution.py:14
  81.9 17.1 %collective-permute-start.11 = (f32[2,1,16,128]{3,2,1,0:T(8,128)S(1)}, f32[2,1,16,128]{3,2,1,0:T(8,128)S(1)}, u32[]{:S(2)}, u32[]{:S(2)}) collective-permute-start(f32[2,1,16,128]{3,2,1,0:T(8,128)S(1)} %slice.738), channel_id=1, source_target_pairs={{0,8},{8,16},{16,24},{1,9},{9,17},{17,25},{2,10},{10,18},{18,26},{... | collective-permute-start | bytes 49160 | tf_op jit(solution)/shard_map/ppermute | solution.py:14
  86.2 12.8 %collective-permute-start.10 = (f32[2,4,16,1]{3,2,1,0:T(8,128)S(1)}, f32[2,4,16,1]{3,2,1,0:T(8,128)S(1)}, u32[]{:S(2)}, u32[]{:S(2)}) collective-permute-start(f32[2,4,16,1]{3,2,1,0:T(8,128)S(1)} %slice.732), channel_id=1, source_target_pairs={{0,1},{1,2},{2,3},{4,5},{5,6},{6,7},{8,9},{9,10},{10,11},{12,13},{... | collective-permute-start | bytes 1544 | tf_op jit(solution)/shard_map/ppermute | solution.py:14
  99.3 11.8 %collective-permute-start.12 = (f32[2,4,1,128]{3,2,1,0:T(1,128)S(1)}, f32[2,4,1,128]{3,2,1,0:T(1,128)S(1)}, u32[]{:S(2)}, u32[]{:S(2)}) collective-permute-start(f32[2,4,1,128]{3,2,1,0:T(1,128)S(1)} %slice.592), channel_id=1, source_target_pairs={{4,0},{5,1},{6,2},{7,3},{12,8},{13,9},{14,10},{15,11},{20,16},{21,... | collective-permute-start | bytes 12296 | tf_op jit(solution)/shard_map/ppermute | solution.py:14
  100.6 10.6 %collective-permute-start.14 = (f32[2,1,16,128]{3,2,1,0:T(8,128)S(1)}, f32[2,1,16,128]{3,2,1,0:T(8,128)S(1)}, u32[]{:S(2)}, u32[]{:S(2)}) collective-permute-start(f32[2,1,16,128]{3,2,1,0:T(8,128)S(1)} %slice.756), channel_id=1, source_target_pairs={{8,0},{16,8},{24,16},{9,1},{17,9},{25,17},{10,2},{18,10},{26,18},{... | collective-permute-start | bytes 49160 | tf_op jit(solution)/shard_map/ppermute | solution.py:14
  101.9 9.2 %collective-permute-start.13 = (f32[2,4,16,1]{3,2,1,0:T(8,128)S(1)}, f32[2,4,16,1]{3,2,1,0:T(8,128)S(1)}, u32[]{:S(2)}, u32[]{:S(2)}) collective-permute-start(f32[2,4,16,1]{3,2,1,0:T(8,128)S(1)} %slice.750), channel_id=1, source_target_pairs={{1,0},{2,1},{3,2},{5,4},{6,5},{7,6},{9,8},{10,9},{11,10},{13,12},{... | collective-permute-start | bytes 1544 | tf_op jit(solution)/shard_map/ppermute | solution.py:14
  111.5 20.4 %collective-permute-start.15 = (f32[2,4,1,128]{3,2,1,0:T(1,128)S(1)}, f32[2,4,1,128]{3,2,1,0:T(1,128)S(1)}, u32[]{:S(2)}, u32[]{:S(2)}) collective-permute-start(f32[2,4,1,128]{3,2,1,0:T(1,128)S(1)} %slice.609), channel_id=1, source_target_pairs={{0,4},{1,5},{2,6},{3,7},{8,12},{9,13},{10,14},{11,15},{16,20},{17,... | collective-permute-start | bytes 12296 | tf_op jit(solution)/shard_map/ppermute | solution.py:14
  114.5 17.3 %collective-permute-start.17 = (f32[2,1,16,128]{3,2,1,0:T(8,128)S(1)}, f32[2,1,16,128]{3,2,1,0:T(8,128)S(1)}, u32[]{:S(2)}, u32[]{:S(2)}) collective-permute-start(f32[2,1,16,128]{3,2,1,0:T(8,128)S(1)} %slice.772), channel_id=1, source_target_pairs={{0,8},{8,16},{16,24},{1,9},{9,17},{17,25},{2,10},{10,18},{18,26},{... | collective-permute-start | bytes 49160 | tf_op jit(solution)/shard_map/ppermute | solution.py:14
  118.8 13.0 %collective-permute-start.16 = (f32[2,4,16,1]{3,2,1,0:T(8,128)S(1)}, f32[2,4,16,1]{3,2,1,0:T(8,128)S(1)}, u32[]{:S(2)}, u32[]{:S(2)}) collective-permute-start(f32[2,4,16,1]{3,2,1,0:T(8,128)S(1)} %slice.766), channel_id=1, source_target_pairs={{0,1},{1,2},{2,3},{4,5},{5,6},{6,7},{8,9},{9,10},{10,11},{12,13},{... | collective-permute-start | bytes 1544 | tf_op jit(solution)/shard_map/ppermute | solution.py:14
  132.2 11.8 %collective-permute-start.18 = (f32[2,4,1,128]{3,2,1,0:T(1,128)S(1)}, f32[2,4,1,128]{3,2,1,0:T(1,128)S(1)}, u32[]{:S(2)}, u32[]{:S(2)}) collective-permute-start(f32[2,4,1,128]{3,2,1,0:T(1,128)S(1)} %slice.628), channel_id=1, source_target_pairs={{4,0},{5,1},{6,2},{7,3},{12,8},{13,9},{14,10},{15,11},{20,16},{21,... | collective-permute-start | bytes 12296 | tf_op jit(solution)/shard_map/ppermute | solution.py:14
  133.5 10.6 %collective-permute-start.20 = (f32[2,1,16,128]{3,2,1,0:T(8,128)S(1)}, f32[2,1,16,128]{3,2,1,0:T(8,128)S(1)}, u32[]{:S(2)}, u32[]{:S(2)}) collective-permute-start(f32[2,1,16,128]{3,2,1,0:T(8,128)S(1)} %slice.790), channel_id=1, source_target_pairs={{8,0},{16,8},{24,16},{9,1},{17,9},{25,17},{10,2},{18,10},{26,18},{... | collective-permute-start | bytes 49160 | tf_op jit(solution)/shard_map/ppermute | solution.py:14
  134.8 9.2 %collective-permute-start.19 = (f32[2,4,16,1]{3,2,1,0:T(8,128)S(1)}, f32[2,4,16,1]{3,2,1,0:T(8,128)S(1)}, u32[]{:S(2)}, u32[]{:S(2)}) collective-permute-start(f32[2,4,16,1]{3,2,1,0:T(8,128)S(1)} %slice.784), channel_id=1, source_target_pairs={{1,0},{2,1},{3,2},{5,4},{6,5},{7,6},{9,8},{10,9},{11,10},{13,12},{... | collective-permute-start | bytes 1544 | tf_op jit(solution)/shard_map/ppermute | solution.py:14
  144.2 23.4 %copy-start.1 = (f32[3,4,16,128]{3,2,1,0:T(8,128)}, f32[3,4,16,128]{3,2,1,0:T(8,128)S(1)}, u32[]{:S(2)}) copy-start(f32[3,4,16,128]{3,2,1,0:T(8,128)S(1)} %fusion.12) | copy-start | bytes 294916
  144.4 20.4 %collective-permute-start.21 = (f32[2,4,1,128]{3,2,1,0:T(1,128)S(1)}, f32[2,4,1,128]{3,2,1,0:T(1,128)S(1)}, u32[]{:S(2)}, u32[]{:S(2)}) collective-permute-start(f32[2,4,1,128]{3,2,1,0:T(1,128)S(1)} %slice.645), channel_id=1, source_target_pairs={{0,4},{1,5},{2,6},{3,7},{8,12},{9,13},{10,14},{11,15},{16,20},{17,... | collective-permute-start | bytes 12296 | tf_op jit(solution)/shard_map/ppermute | solution.py:14
  147.4 17.3 %collective-permute-start.23 = (f32[2,1,16,128]{3,2,1,0:T(8,128)S(1)}, f32[2,1,16,128]{3,2,1,0:T(8,128)S(1)}, u32[]{:S(2)}, u32[]{:S(2)}) collective-permute-start(f32[2,1,16,128]{3,2,1,0:T(8,128)S(1)} %slice.806), channel_id=1, source_target_pairs={{0,8},{8,16},{16,24},{1,9},{9,17},{17,25},{2,10},{10,18},{18,26},{... | collective-permute-start | bytes 49160 | tf_op jit(solution)/shard_map/ppermute | solution.py:14
  151.7 13.0 %collective-permute-start.22 = (f32[2,4,16,1]{3,2,1,0:T(8,128)S(1)}, f32[2,4,16,1]{3,2,1,0:T(8,128)S(1)}, u32[]{:S(2)}, u32[]{:S(2)}) collective-permute-start(f32[2,4,16,1]{3,2,1,0:T(8,128)S(1)} %slice.800), channel_id=1, source_target_pairs={{0,1},{1,2},{2,3},{4,5},{5,6},{6,7},{8,9},{9,10},{10,11},{12,13},{... | collective-permute-start | bytes 1544 | tf_op jit(solution)/shard_map/ppermute | solution.py:14
  164.9 25.7 %copy-start.4 = (f32[3,4,16,128]{3,2,1,0:T(8,128)}, f32[3,4,16,128]{3,2,1,0:T(8,128)S(1)}, u32[]{:S(2)}) copy-start(f32[3,4,16,128]{3,2,1,0:T(8,128)S(1)} %fusion.14) | copy-start | bytes 294916
  180.2 9.4 %all-to-all-start = ((f32[3,192,8]{1,0,2:T(4,128)}), f32[3,192,8]{1,0,2:T(4,128)S(1)}, u32[]{:S(2)}, u32[]{:S(2)}) async-start(f32[3,192,8]{1,0,2:T(4,128)} %bitcast.97), calls=%async_computation | async-start | bytes 65536 | tf_op jit(solution)/shard_map/all_to_all | solution.py:125
where the time goes:
time: 193 us; the launch traced here: 191 us
  local copies, waits for them, and re-layouts  83.1 us (43%)
  starting transfers between devices  74.3 us (38%)
  other arithmetic  23.8 us (12%)
  waiting for transfers between devices  5.8 us (3%)
  between operations  2.54 us (1%)
    ppermute x24, starting transfers between devices, passed_along(): return lax.ppermute(shard, axis, pairs)  62.8 us
    gather x8, local copies, waits for them, and re-layouts, local(): magn_rows = magnetic.reshape(3, -1)[:, slot_cells]  20.7 us
    gather x8, local copies, waits for them, and re-layouts, local(): elec_rows = electric.reshape(3, -1)[:, slot_cells]  20.7 us
    sub x4, local copies, waits for them, and re-layouts, local(): magnetic = magnetic - STEP_DT * curl_upper(electric)  10.5 us
    add x4, local copies, waits for them, and re-layouts, local(): electric = keep_e * electric + gain_e * (curl_magn - drude)  10.5 us
    unnamed x15, local copies, waits for them, and re-layouts  9.26 us
    all_to_all x1, starting transfers between devices, local(): lax.all_to_all(tile_buf, ('gx', 'gy'), split_axis=2, concat_axis=2, tiled...  7.86 us
    all_to_all x1, waiting for transfers between devices, local(): lax.all_to_all(force_buf, ('gx', 'gy'), split_axis=2, concat_axis=2, tile...  5.74 us
  transfers between devices with their start and end apart: 26, of which 1 were waited for; matrix products, arithmetic and copies ran while one was open for 56% of the time, Pallas kernels for 0%

commit v1 on v0

--- a/solution.py
+++ b/solution.py
@@ -122,7 +122,15 @@
         .set(tile_ids.astype(jnp.float32))
     )
     got_force, got_tile = (
-        lax.all_to_all(force_buf, ("gx", "gy"), split_axis=2, concat_axis=2, tiled=True),
+        jnp.concatenate(
+            lax.all_to_all(
+                jnp.stack(jnp.split(force_buf, lax.axis_size(("gx", "gy")), axis=2)),
+                ("gx", "gy"),
+                0,
+                0,
+            ),
+            axis=2,
+        ),
         lax.all_to_all(tile_buf, ("gx", "gy"), split_axis=2, concat_axis=2, tiled=True),
     )
     tile_hot = (

time: 193 us -> 197 us (1.021)
  local copies, waits for them, and re-layouts: 83.1 us -> 87.3 us
    unnamed x15 -> x22, local copies, waits for them, and re-layouts: 9.26 us -> 12.8 us
  transfers between devices with their start and end apart: 26 -> 26, of which waited for: 1 -> 1; matrix products, arithmetic and copies ran while one was open for 56% -> 57% of each run, Pallas kernels for 0% -> 0%
where the time goes in v1:
time: 197 us; the launch traced here: 195 us
  local copies, waits for them, and re-layouts  87.3 us (44%)
  starting transfers between devices  74.3 us (38%)
  other arithmetic  23.8 us (12%)
  waiting for transfers between devices  5.76 us (3%)
  between operations  2.54 us (1%)
    ppermute x24, starting transfers between devices, passed_along(): return lax.ppermute(shard, axis, pairs)  62.8 us
    gather x8, local copies, waits for them, and re-layouts, local(): magn_rows = magnetic.reshape(3, -1)[:, slot_cells]  20.7 us
    gather x8, local copies, waits for them, and re-layouts, local(): elec_rows = electric.reshape(3, -1)[:, slot_cells]  20.7 us
    unnamed x22, local copies, waits for them, and re-layouts  12.8 us
    sub x4, local copies, waits for them, and re-layouts, local(): magnetic = magnetic - STEP_DT * curl_upper(electric)  10.5 us
    add x4, local copies, waits for them, and re-layouts, local(): electric = keep_e * electric + gain_e * (curl_magn - drude)  10.5 us
    all_to_all x1, starting transfers between devices, local(): lax.all_to_all(tile_buf, ('gx', 'gy'), split_axis=2, concat_axis=2, tiled...  7.86 us
    div x1, other arithmetic, coefficients(): gain_e = STEP_DT / (1.0 + sigma * STEP_DT / 2)  5.73 us
  transfers between devices with their start and end apart: 26, of which 1 were waited for; matrix products, arithmetic and copies ran while one was open for 57% of the time, Pallas kernels for 0%

profile of v1, /device:TPU:0, one launch (start us, length us, event | category | flops | bytes accessed | tf_op | source)
XLA Modules:
  0.0 194.7 jit_solution(9833098334722205153)
XLA Ops:
  11.8 4.3 %scatter_custom_fusion.1 = f32[1536]{0:T(1024)S(1)} fusion(s32[1024]{0:T(1024)S(1)} %broadcast_select_fusion, f32[1024]{0:T(1024)S(1)} %bitcast.355, f32[]{:T(128)} %constant.91.clone.1), kind=kCustom, calls=%fused_computation.273 | custom fusion | bytes 6148
  16.8 7.9 %all-to-all-start.1 = ((f32[1,192,8]{1,0,2:T(1,128)}), f32[1,192,8]{1,0,2:T(1,128)S(1)}, u32[]{:S(2)}, u32[]{:S(2)}) async-start(f32[1,192,8]{1,0,2:T(1,128)} %bitcast.109), calls=%async_computation.1 | async-start | bytes 16384 | tf_op jit(solution)/shard_map/all_to_all | solution.py:134
  37.7 2.7 %subtract_divide_fusion.1 = (f32[4,16,128]{2,1,0:T(8,128)S(1)}, pred[4,16,128]{2,1,0:T(8,128)(4,1)S(1)}, pred[4,16,128]{2,1,0:T(8,128)(4,1)S(1)}, pred[4,16,128]{2,1,0:T(8,128)(4,1)S(1)}) fusion(f32[]{:T(128)} %bitcast.2, f32[]{:T(128)} %bitcast.1, f32[]{:T(128)} %bitcast, s32[4,16,128]{2,1,0:T(8,128)} %param.16), kind=kLoop, calls=%fused_computation.154 | loop fusion | flops 98304 | bytes 90124 | tf_op jit(solution)/shard_map/div | solution.py:28
  40.4 5.7 %add_divide_fusion = (f32[4,16,128]{2,1,0:T(8,128)S(1)}, f32[4,16,128]{2,1,0:T(8,128)S(1)}, f32[4,16,128]{2,1,0:T(8,128)S(1)}) fusion(pred[4,16,128]{2,1,0:T(8,128)(4,1)S(1)} %get-tuple-element.38, pred[4,16,128]{2,1,0:T(8,128)(4,1)S(1)} %get-tuple-element.37, pred[4,16,128]{2,1,0:T(8,128)(4,1)S(1)} %get-tuple-element.36, f32[]{:T(128)} %bitcast.2, ...), kind=kLoop, calls=%fused_computation.157 | loop fusion | flops 196608 | bytes 122916 | tf_op jit(solution)/shard_map/div | solution.py:29
  50.6 3.5 %collective-permute-start.5 = (f32[2,1,16,128]{3,2,1,0:T(8,128)S(1)}, f32[2,1,16,128]{3,2,1,0:T(8,128)S(1)}, u32[]{:S(2)}, u32[]{:S(2)}) collective-permute-start(f32[2,1,16,128]{3,2,1,0:T(8,128)S(1)} %slice.704), channel_id=1, source_target_pairs={{0,8},{8,16},{16,24},{1,9},{9,17},{17,25},{2,10},{10,18},{18,26},{... | collective-permute-start | bytes 49160 | tf_op jit(solution)/shard_map/ppermute | solution.py:14
  54.2 4.3 %collective-permute-start.4 = (f32[2,4,16,1]{3,2,1,0:T(8,128)S(1)}, f32[2,4,16,1]{3,2,1,0:T(8,128)S(1)}, u32[]{:S(2)}, u32[]{:S(2)}) collective-permute-start(f32[2,4,16,1]{3,2,1,0:T(8,128)S(1)} %slice.698), channel_id=1, source_target_pairs={{0,1},{1,2},{2,3},{4,5},{5,6},{6,7},{8,9},{9,10},{10,11},{12,13},{... | collective-permute-start | bytes 1544 | tf_op jit(solution)/shard_map/ppermute | solution.py:14
  58.5 2.6 %copy.60 = f32[3,4,16,128]{0,3,2,1:T(8,128)} copy(f32[3,4,16,128]{3,2,1,0:T(8,128)S(1)} %fusion.3) | data formatting | bytes 196608 | tf_op jit(solution)/shard_map/sub | solution.py:106
  61.1 5.0 %gather_fusion.1 = f32[1024,3]{1,0:T(8,128)S(1)} fusion(f32[3,8192]{0,1:T(8,128)} %bitcast.331, s32[1024]{0:T(1024)S(1)} %broadcast_clamp_fusion), kind=kCustom, calls=%fused_computation.1 | custom fusion | bytes 28672 | tf_op jit(solution)/shard_map/gather | solution.py:111
  70.7 2.6 %copy.58 = f32[3,4,16,128]{0,3,2,1:T(8,128)} copy(f32[3,4,16,128]{3,2,1,0:T(8,128)S(1)} %fusion.5) | data formatting | bytes 196608 | tf_op jit(solution)/shard_map/add | solution.py:109
  73.3 5.0 %gather_fusion = f32[1024,3]{1,0:T(8,128)S(1)} fusion(f32[3,8192]{0,1:T(8,128)} %bitcast.332, s32[1024]{0:T(1024)S(1)} %broadcast_clamp_fusion), kind=kCustom, calls=%fused_computation | custom fusion | bytes 28672 | tf_op jit(solution)/shard_map/gather | solution.py:110
  78.9 3.0 %collective-permute-start.9 = (f32[2,4,1,128]{3,2,1,0:T(1,128)S(1)}, f32[2,4,1,128]{3,2,1,0:T(1,128)S(1)}, u32[]{:S(2)}, u32[]{:S(2)}) collective-permute-start(f32[2,4,1,128]{3,2,1,0:T(1,128)S(1)} %slice.573), channel_id=1, source_target_pairs={{0,4},{1,5},{2,6},{3,7},{8,12},{9,13},{10,14},{11,15},{16,20},{17,... | collective-permute-start | bytes 12296 | tf_op jit(solution)/shard_map/ppermute | solution.py:14
  81.9 4.3 %collective-permute-start.11 = (f32[2,1,16,128]{3,2,1,0:T(8,128)S(1)}, f32[2,1,16,128]{3,2,1,0:T(8,128)S(1)}, u32[]{:S(2)}, u32[]{:S(2)}) collective-permute-start(f32[2,1,16,128]{3,2,1,0:T(8,128)S(1)} %slice.738), channel_id=1, source_target_pairs={{0,8},{8,16},{16,24},{1,9},{9,17},{17,25},{2,10},{10,18},{18,26},{... | collective-permute-start | bytes 49160 | tf_op jit(solution)/shard_map/ppermute | solution.py:14
  86.2 4.9 %collective-permute-start.10 = (f32[2,4,16,1]{3,2,1,0:T(8,128)S(1)}, f32[2,4,16,1]{3,2,1,0:T(8,128)S(1)}, u32[]{:S(2)}, u32[]{:S(2)}) collective-permute-start(f32[2,4,16,1]{3,2,1,0:T(8,128)S(1)} %slice.732), channel_id=1, source_target_pairs={{0,1},{1,2},{2,3},{4,5},{5,6},{6,7},{8,9},{9,10},{10,11},{12,13},{... | collective-permute-start | bytes 1544 | tf_op jit(solution)/shard_map/ppermute | solution.py:14
  91.1 2.6 %copy.64 = f32[3,4,16,128]{0,3,2,1:T(8,128)} copy(f32[3,4,16,128]{3,2,1,0:T(8,128)S(1)} %fusion.6) | data formatting | bytes 196608 | tf_op jit(solution)/shard_map/sub | solution.py:106
  93.8 5.0 %gather_fusion.3 = f32[1024,3]{1,0:T(8,128)S(1)} fusion(f32[3,8192]{0,1:T(8,128)} %bitcast.333, s32[1024]{0:T(1024)S(1)} %broadcast_clamp_fusion), kind=kCustom, calls=%fused_computation.3 | custom fusion | bytes 28672 | tf_op jit(solution)/shard_map/gather | solution.py:111
  106.0 5.0 %gather_fusion.2 = f32[1024,3]{1,0:T(8,128)S(1)} fusion(f32[3,8192]{0,1:T(8,128)} %bitcast.334, s32[1024]{0:T(1024)S(1)} %broadcast_clamp_fusion), kind=kCustom, calls=%fused_computation.2 | custom fusion | bytes 28672 | tf_op jit(solution)/shard_map/gather | solution.py:110
  111.5 3.0 %collective-permute-start.15 = (f32[2,4,1,128]{3,2,1,0:T(1,128)S(1)}, f32[2,4,1,128]{3,2,1,0:T(1,128)S(1)}, u32[]{:S(2)}, u32[]{:S(2)}) collective-permute-start(f32[2,4,1,128]{3,2,1,0:T(1,128)S(1)} %slice.609), channel_id=1, source_target_pairs={{0,4},{1,5},{2,6},{3,7},{8,12},{9,13},{10,14},{11,15},{16,20},{17,... | collective-permute-start | bytes 12296 | tf_op jit(solution)/shard_map/ppermute | solution.py:14
  114.5 4.3 %collective-permute-start.17 = (f32[2,1,16,128]{3,2,1,0:T(8,128)S(1)}, f32[2,1,16,128]{3,2,1,0:T(8,128)S(1)}, u32[]{:S(2)}, u32[]{:S(2)}) collective-permute-start(f32[2,1,16,128]{3,2,1,0:T(8,128)S(1)} %slice.772), channel_id=1, source_target_pairs={{0,8},{8,16},{16,24},{1,9},{9,17},{17,25},{2,10},{10,18},{18,26},{... | collective-permute-start | bytes 49160 | tf_op jit(solution)/shard_map/ppermute | solution.py:14
  118.8 5.2 %collective-permute-start.16 = (f32[2,4,16,1]{3,2,1,0:T(8,128)S(1)}, f32[2,4,16,1]{3,2,1,0:T(8,128)S(1)}, u32[]{:S(2)}, u32[]{:S(2)}) collective-permute-start(f32[2,4,16,1]{3,2,1,0:T(8,128)S(1)} %slice.766), channel_id=1, source_target_pairs={{0,1},{1,2},{2,3},{4,5},{5,6},{6,7},{8,9},{9,10},{10,11},{12,13},{... | collective-permute-start | bytes 1544 | tf_op jit(solution)/shard_map/ppermute | solution.py:14
  124.0 2.6 %copy.68 = f32[3,4,16,128]{0,3,2,1:T(8,128)} copy(f32[3,4,16,128]{3,2,1,0:T(8,128)S(1)} %fusion.9) | data formatting | bytes 196608 | tf_op jit(solution)/shard_map/sub | solution.py:106
  126.6 5.0 %gather_fusion.5 = f32[1024,3]{1,0:T(8,128)S(1)} fusion(f32[3,8192]{0,1:T(8,128)} %bitcast.335, s32[1024]{0:T(1024)S(1)} %broadcast_clamp_fusion), kind=kCustom, calls=%fused_computation.5 | custom fusion | bytes 28672 | tf_op jit(solution)/shard_map/gather | solution.py:111
  136.2 2.6 %copy.66 = f32[3,4,16,128]{0,3,2,1:T(8,128)} copy(f32[3,4,16,128]{3,2,1,0:T(8,128)S(1)} %fusion.11) | data formatting | bytes 196608 | tf_op jit(solution)/shard_map/add | solution.py:109
  138.8 5.0 %gather_fusion.4 = f32[1024,3]{1,0:T(8,128)S(1)} fusion(f32[3,8192]{0,1:T(8,128)} %bitcast.336, s32[1024]{0:T(1024)S(1)} %broadcast_clamp_fusion), kind=kCustom, calls=%fused_computation.4 | custom fusion | bytes 28672 | tf_op jit(solution)/shard_map/gather | solution.py:110
  144.4 3.0 %collective-permute-start.21 = (f32[2,4,1,128]{3,2,1,0:T(1,128)S(1)}, f32[2,4,1,128]{3,2,1,0:T(1,128)S(1)}, u32[]{:S(2)}, u32[]{:S(2)}) collective-permute-start(f32[2,4,1,128]{3,2,1,0:T(1,128)S(1)} %slice.645), channel_id=1, source_target_pairs={{0,4},{1,5},{2,6},{3,7},{8,12},{9,13},{10,14},{11,15},{16,20},{17,... | collective-permute-start | bytes 12296 | tf_op jit(solution)/shard_map/ppermute | solution.py:14
  147.4 4.3 %collective-permute-start.23 = (f32[2,1,16,128]{3,2,1,0:T(8,128)S(1)}, f32[2,1,16,128]{3,2,1,0:T(8,128)S(1)}, u32[]{:S(2)}, u32[]{:S(2)}) collective-permute-start(f32[2,1,16,128]{3,2,1,0:T(8,128)S(1)} %slice.806), channel_id=1, source_target_pairs={{0,8},{8,16},{16,24},{1,9},{9,17},{17,25},{2,10},{10,18},{18,26},{... | collective-permute-start | bytes 49160 | tf_op jit(solution)/shard_map/ppermute | solution.py:14
  151.7 5.2 %collective-permute-start.22 = (f32[2,4,16,1]{3,2,1,0:T(8,128)S(1)}, f32[2,4,16,1]{3,2,1,0:T(8,128)S(1)}, u32[]{:S(2)}, u32[]{:S(2)}) collective-permute-start(f32[2,4,16,1]{3,2,1,0:T(8,128)S(1)} %slice.800), channel_id=1, source_target_pairs={{0,1},{1,2},{2,3},{4,5},{5,6},{6,7},{8,9},{9,10},{10,11},{12,13},{... | collective-permute-start | bytes 1544 | tf_op jit(solution)/shard_map/ppermute | solution.py:14
  159.5 5.0 %gather_fusion.7 = f32[1024,3]{1,0:T(8,128)S(1)} fusion(f32[3,8192]{0,1:T(8,128)} %bitcast.337, s32[1024]{0:T(1024)S(1)} %broadcast_clamp_fusion), kind=kCustom, calls=%fused_computation.7 | custom fusion | bytes 28672 | tf_op jit(solution)/shard_map/gather | solution.py:111
  167.6 5.0 %gather_fusion.6 = f32[1024,3]{1,0:T(8,128)S(1)} fusion(f32[3,8192]{0,1:T(8,128)} %bitcast.330, s32[1024]{0:T(1024)S(1)} %broadcast_clamp_fusion), kind=kCustom, calls=%fused_computation.6 | custom fusion | bytes 28672 | tf_op jit(solution)/shard_map/gather | solution.py:110
  173.0 2.7 %fusion.52 = f32[1024,3]{0,1:T(4,128)S(1)} fusion(f32[1024,3]{0,1:T(4,128)S(1)} %copy.73, f32[1024,3]{0,1:T(4,128)S(1)} %copy.71, f32[1024,3]{0,1:T(4,128)S(1)} %copy.69, f32[1024,3]{0,1:T(4,128)S(1)} %copy.67, f32[1024,3]{0,1:T(4,128)S(1)} %copy.65, f32[1024,3]{0,1:T(4,128)S(1)} %copy.63, f32[1024,3]{0,1:T(4,128)S(1)} %copy.61, f32[1024,3]{0,1:T(4,128)S(1)} %copy.59, ...), kind=kLoop, calls=%fused_computation.205 | loop fusion | flops 101376 | bytes 172048 | tf_op jit(solution)/shard_map/mul | solution.py:113
  175.9 3.3 %scatter_custom_fusion = f32[3,1536]{0,1:T(8,128)S(1)} fusion(s32[1024]{0:T(1024)S(1)} %broadcast_select_fusion.1, f32[1024,3]{1,0:T(8,128)S(1)} %copy.74, f32[]{:T(128)} %constant.82.clone.1), kind=kCustom, calls=%fused_computation.12 | custom fusion | bytes 18436
  184.3 3.6 %all-to-all-start = ((f32[8,3,192,1]{2,3,1,0:T(1,128)}), f32[8,3,192,1]{2,3,1,0:T(1,128)S(1)}, u32[]{:S(2)}, u32[]{:S(2)}) async-start(f32[8,3,192,1]{2,3,1,0:T(1,128)} %constant_dynamic-update-slice_fusion), calls=%async_computation | async-start | bytes 49152 | tf_op jit(solution)/shard_map/all_to_all | solution.py:126
  187.9 5.7 %all-to-all-done = f32[8,3,192,1]{2,3,1,0:T(1,128)S(1)} async-done(((f32[8,3,192,1]{2,3,1,0:T(1,128)}), f32[8,3,192,1]{2,3,1,0:T(1,128)S(1)}, u32[]{:S(2)}, u32[]{:S(2)}) %all-to-all-start) | async-done | bytes 18464 | tf_op jit(solution)/shard_map/all_to_all | solution.py:126
  (211 shorter events, 58.2 us)
Async XLA Ops:
  1.4 44.8 %collective-permute-start = (f32[2,4,1,128]{3,2,1,0:T(1,128)S(1)}, f32[2,4,1,128]{3,2,1,0:T(1,128)S(1)}, u32[]{:S(2)}, u32[]{:S(2)}) collective-permute-start(f32[2,4,1,128]{3,2,1,0:T(1,128)S(1)} %slice.514), channel_id=1, source_target_pairs={{4,0},{5,1},{6,2},{7,3},{12,8},{13,9},{14,10},{15,11},{20,16},{21,... | collective-permute-start | bytes 12296 | tf_op jit(solution)/shard_map/ppermute | solution.py:14
  3.4 42.8 %collective-permute-start.2 = (f32[2,1,16,128]{3,2,1,0:T(8,128)S(1)}, f32[2,1,16,128]{3,2,1,0:T(8,128)S(1)}, u32[]{:S(2)}, u32[]{:S(2)}) collective-permute-start(f32[2,1,16,128]{3,2,1,0:T(8,128)S(1)} %slice.524), channel_id=1, source_target_pairs={{8,0},{16,8},{24,16},{9,1},{17,9},{25,17},{10,2},{18,10},{26,18},{... | collective-permute-start | bytes 49160 | tf_op jit(solution)/shard_map/ppermute | solution.py:14
  16.8 167.5 %all-to-all-start.1 = ((f32[1,192,8]{1,0,2:T(1,128)}), f32[1,192,8]{1,0,2:T(1,128)S(1)}, u32[]{:S(2)}, u32[]{:S(2)}) async-start(f32[1,192,8]{1,0,2:T(1,128)} %bitcast.109), calls=%async_computation.1 | async-start | bytes 16384 | tf_op jit(solution)/shard_map/all_to_all | solution.py:134
  24.7 41.8 %copy-start = (f32[3,4,16,128]{3,2,1,0:T(8,128)S(1)}, f32[3,4,16,128]{3,2,1,0:T(8,128)}, u32[]{:S(2)}) copy-start(f32[3,4,16,128]{3,2,1,0:T(8,128)} %param.13) | copy-start | bytes 294916
  24.7 41.8 %copy-start.3 = (f32[3,4,16,128]{3,2,1,0:T(8,128)S(1)}, f32[3,4,16,128]{3,2,1,0:T(8,128)}, u32[]{:S(2)}) copy-start(f32[3,4,16,128]{3,2,1,0:T(8,128)} %param.15) | copy-start | bytes 294916
  25.6 20.6 %collective-permute-start.1 = (f32[2,4,16,1]{3,2,1,0:T(8,128)S(1)}, f32[2,4,16,1]{3,2,1,0:T(8,128)S(1)}, u32[]{:S(2)}, u32[]{:S(2)}) collective-permute-start(f32[2,4,16,1]{3,2,1,0:T(8,128)S(1)} %slice.518), channel_id=1, source_target_pairs={{1,0},{2,1},{3,2},{5,4},{6,5},{7,6},{9,8},{10,9},{11,10},{13,12},{... | collective-permute-start | bytes 1544 | tf_op jit(solution)/shard_map/ppermute | solution.py:14
  48.2 18.1 %collective-permute-start.3 = (f32[2,4,1,128]{3,2,1,0:T(1,128)S(1)}, f32[2,4,1,128]{3,2,1,0:T(1,128)S(1)}, u32[]{:S(2)}, u32[]{:S(2)}) collective-permute-start(f32[2,4,1,128]{3,2,1,0:T(1,128)S(1)} %slice.531), channel_id=1, source_target_pairs={{0,4},{1,5},{2,6},{3,7},{8,12},{9,13},{10,14},{11,15},{16,20},{17,... | collective-permute-start | bytes 12296 | tf_op jit(solution)/shard_map/ppermute | solution.py:14
  50.6 15.7 %collective-permute-start.5 = (f32[2,1,16,128]{3,2,1,0:T(8,128)S(1)}, f32[2,1,16,128]{3,2,1,0:T(8,128)S(1)}, u32[]{:S(2)}, u32[]{:S(2)}) collective-permute-start(f32[2,1,16,128]{3,2,1,0:T(8,128)S(1)} %slice.704), channel_id=1, source_target_pairs={{0,8},{8,16},{16,24},{1,9},{9,17},{17,25},{2,10},{10,18},{18,26},{... | collective-permute-start | bytes 49160 | tf_op jit(solution)/shard_map/ppermute | solution.py:14
  54.2 12.2 %collective-permute-start.4 = (f32[2,4,16,1]{3,2,1,0:T(8,128)S(1)}, f32[2,4,16,1]{3,2,1,0:T(8,128)S(1)}, u32[]{:S(2)}, u32[]{:S(2)}) collective-permute-start(f32[2,4,16,1]{3,2,1,0:T(8,128)S(1)} %slice.698), channel_id=1, source_target_pairs={{0,1},{1,2},{2,3},{4,5},{5,6},{6,7},{8,9},{9,10},{10,11},{12,13},{... | collective-permute-start | bytes 1544 | tf_op jit(solution)/shard_map/ppermute | solution.py:14
  61.1 17.6 %copy-start.2 = (f32[3,4,16,128]{3,2,1,0:T(8,128)S(1)}, f32[3,4,16,128]{3,2,1,0:T(8,128)}, u32[]{:S(2)}) copy-start(f32[3,4,16,128]{3,2,1,0:T(8,128)} %param.14) | copy-start | bytes 294916
  66.7 11.8 %collective-permute-start.6 = (f32[2,4,1,128]{3,2,1,0:T(1,128)S(1)}, f32[2,4,1,128]{3,2,1,0:T(1,128)S(1)}, u32[]{:S(2)}, u32[]{:S(2)}) collective-permute-start(f32[2,4,1,128]{3,2,1,0:T(1,128)S(1)} %slice.556), channel_id=1, source_target_pairs={{4,0},{5,1},{6,2},{7,3},{12,8},{13,9},{14,10},{15,11},{20,16},{21,... | collective-permute-start | bytes 12296 | tf_op jit(solution)/shard_map/ppermute | solution.py:14
  68.0 10.6 %collective-permute-start.8 = (f32[2,1,16,128]{3,2,1,0:T(8,128)S(1)}, f32[2,1,16,128]{3,2,1,0:T(8,128)S(1)}, u32[]{:S(2)}, u32[]{:S(2)}) collective-permute-start(f32[2,1,16,128]{3,2,1,0:T(8,128)S(1)} %slice.722), channel_id=1, source_target_pairs={{8,0},{16,8},{24,16},{9,1},{17,9},{25,17},{10,2},{18,10},{26,18},{... | collective-permute-start | bytes 49160 | tf_op jit(solution)/shard_map/ppermute | solution.py:14
  69.3 9.2 %collective-permute-start.7 = (f32[2,4,16,1]{3,2,1,0:T(8,128)S(1)}, f32[2,4,16,1]{3,2,1,0:T(8,128)S(1)}, u32[]{:S(2)}, u32[]{:S(2)}) collective-permute-start(f32[2,4,16,1]{3,2,1,0:T(8,128)S(1)} %slice.716), channel_id=1, source_target_pairs={{1,0},{2,1},{3,2},{5,4},{6,5},{7,6},{9,8},{10,9},{11,10},{13,12},{... | collective-permute-start | bytes 1544 | tf_op jit(solution)/shard_map/ppermute | solution.py:14
  78.9 20.1 %collective-permute-start.9 = (f32[2,4,1,128]{3,2,1,0:T(1,128)S(1)}, f32[2,4,1,128]{3,2,1,0:T(1,128)S(1)}, u32[]{:S(2)}, u32[]{:S(2)}) collective-permute-start(f32[2,4,1,128]{3,2,1,0:T(1,128)S(1)} %slice.573), channel_id=1, source_target_pairs={{0,4},{1,5},{2,6},{3,7},{8,12},{9,13},{10,14},{11,15},{16,20},{17,... | collective-permute-start | bytes 12296 | tf_op jit(solution)/shard_map/ppermute | solution.py:14
  81.9 17.1 %collective-permute-start.11 = (f32[2,1,16,128]{3,2,1,0:T(8,128)S(1)}, f32[2,1,16,128]{3,2,1,0:T(8,128)S(1)}, u32[]{:S(2)}, u32[]{:S(2)}) collective-permute-start(f32[2,1,16,128]{3,2,1,0:T(8,128)S(1)} %slice.738), channel_id=1, source_target_pairs={{0,8},{8,16},{16,24},{1,9},{9,17},{17,25},{2,10},{10,18},{18,26},{... | collective-permute-start | bytes 49160 | tf_op jit(solution)/shard_map/ppermute | solution.py:14
  86.2 12.8 %collective-permute-start.10 = (f32[2,4,16,1]{3,2,1,0:T(8,128)S(1)}, f32[2,4,16,1]{3,2,1,0:T(8,128)S(1)}, u32[]{:S(2)}, u32[]{:S(2)}) collective-permute-start(f32[2,4,16,1]{3,2,1,0:T(8,128)S(1)} %slice.732), channel_id=1, source_target_pairs={{0,1},{1,2},{2,3},{4,5},{5,6},{6,7},{8,9},{9,10},{10,11},{12,13},{... | collective-permute-start | bytes 1544 | tf_op jit(solution)/shard_map/ppermute | solution.py:14
  99.3 11.8 %collective-permute-start.12 = (f32[2,4,1,128]{3,2,1,0:T(1,128)S(1)}, f32[2,4,1,128]{3,2,1,0:T(1,128)S(1)}, u32[]{:S(2)}, u32[]{:S(2)}) collective-permute-start(f32[2,4,1,128]{3,2,1,0:T(1,128)S(1)} %slice.592), channel_id=1, source_target_pairs={{4,0},{5,1},{6,2},{7,3},{12,8},{13,9},{14,10},{15,11},{20,16},{21,... | collective-permute-start | bytes 12296 | tf_op jit(solution)/shard_map/ppermute | solution.py:14
  100.6 10.6 %collective-permute-start.14 = (f32[2,1,16,128]{3,2,1,0:T(8,128)S(1)}, f32[2,1,16,128]{3,2,1,0:T(8,128)S(1)}, u32[]{:S(2)}, u32[]{:S(2)}) collective-permute-start(f32[2,1,16,128]{3,2,1,0:T(8,128)S(1)} %slice.756), channel_id=1, source_target_pairs={{8,0},{16,8},{24,16},{9,1},{17,9},{25,17},{10,2},{18,10},{26,18},{... | collective-permute-start | bytes 49160 | tf_op jit(solution)/shard_map/ppermute | solution.py:14
  101.9 9.2 %collective-permute-start.13 = (f32[2,4,16,1]{3,2,1,0:T(8,128)S(1)}, f32[2,4,16,1]{3,2,1,0:T(8,128)S(1)}, u32[]{:S(2)}, u32[]{:S(2)}) collective-permute-start(f32[2,4,16,1]{3,2,1,0:T(8,128)S(1)} %slice.750), channel_id=1, source_target_pairs={{1,0},{2,1},{3,2},{5,4},{6,5},{7,6},{9,8},{10,9},{11,10},{13,12},{... | collective-permute-start | bytes 1544 | tf_op jit(solution)/shard_map/ppermute | solution.py:14
  111.5 20.4 %collective-permute-start.15 = (f32[2,4,1,128]{3,2,1,0:T(1,128)S(1)}, f32[2,4,1,128]{3,2,1,0:T(1,128)S(1)}, u32[]{:S(2)}, u32[]{:S(2)}) collective-permute-start(f32[2,4,1,128]{3,2,1,0:T(1,128)S(1)} %slice.609), channel_id=1, source_target_pairs={{0,4},{1,5},{2,6},{3,7},{8,12},{9,13},{10,14},{11,15},{16,20},{17,... | collective-permute-start | bytes 12296 | tf_op jit(solution)/shard_map/ppermute | solution.py:14
  114.5 17.3 %collective-permute-start.17 = (f32[2,1,16,128]{3,2,1,0:T(8,128)S(1)}, f32[2,1,16,128]{3,2,1,0:T(8,128)S(1)}, u32[]{:S(2)}, u32[]{:S(2)}) collective-permute-start(f32[2,1,16,128]{3,2,1,0:T(8,128)S(1)} %slice.772), channel_id=1, source_target_pairs={{0,8},{8,16},{16,24},{1,9},{9,17},{17,25},{2,10},{10,18},{18,26},{... | collective-permute-start | bytes 49160 | tf_op jit(solution)/shard_map/ppermute | solution.py:14
  118.8 13.0 %collective-permute-start.16 = (f32[2,4,16,1]{3,2,1,0:T(8,128)S(1)}, f32[2,4,16,1]{3,2,1,0:T(8,128)S(1)}, u32[]{:S(2)}, u32[]{:S(2)}) collective-permute-start(f32[2,4,16,1]{3,2,1,0:T(8,128)S(1)} %slice.766), channel_id=1, source_target_pairs={{0,1},{1,2},{2,3},{4,5},{5,6},{6,7},{8,9},{9,10},{10,11},{12,13},{... | collective-permute-start | bytes 1544 | tf_op jit(solution)/shard_map/ppermute | solution.py:14
  132.2 11.8 %collective-permute-start.18 = (f32[2,4,1,128]{3,2,1,0:T(1,128)S(1)}, f32[2,4,1,128]{3,2,1,0:T(1,128)S(1)}, u32[]{:S(2)}, u32[]{:S(2)}) collective-permute-start(f32[2,4,1,128]{3,2,1,0:T(1,128)S(1)} %slice.628), channel_id=1, source_target_pairs={{4,0},{5,1},{6,2},{7,3},{12,8},{13,9},{14,10},{15,11},{20,16},{21,... | collective-permute-start | bytes 12296 | tf_op jit(solution)/shard_map/ppermute | solution.py:14
  133.5 10.6 %collective-permute-start.20 = (f32[2,1,16,128]{3,2,1,0:T(8,128)S(1)}, f32[2,1,16,128]{3,2,1,0:T(8,128)S(1)}, u32[]{:S(2)}, u32[]{:S(2)}) collective-permute-start(f32[2,1,16,128]{3,2,1,0:T(8,128)S(1)} %slice.790), channel_id=1, source_target_pairs={{8,0},{16,8},{24,16},{9,1},{17,9},{25,17},{10,2},{18,10},{26,18},{... | collective-permute-start | bytes 49160 | tf_op jit(solution)/shard_map/ppermute | solution.py:14
  134.8 9.2 %collective-permute-start.19 = (f32[2,4,16,1]{3,2,1,0:T(8,128)S(1)}, f32[2,4,16,1]{3,2,1,0:T(8,128)S(1)}, u32[]{:S(2)}, u32[]{:S(2)}) collective-permute-start(f32[2,4,16,1]{3,2,1,0:T(8,128)S(1)} %slice.784), channel_id=1, source_target_pairs={{1,0},{2,1},{3,2},{5,4},{6,5},{7,6},{9,8},{10,9},{11,10},{13,12},{... | collective-permute-start | bytes 1544 | tf_op jit(solution)/shard_map/ppermute | solution.py:14
  144.2 23.4 %copy-start.1 = (f32[3,4,16,128]{3,2,1,0:T(8,128)}, f32[3,4,16,128]{3,2,1,0:T(8,128)S(1)}, u32[]{:S(2)}) copy-start(f32[3,4,16,128]{3,2,1,0:T(8,128)S(1)} %fusion.12) | copy-start | bytes 294916
  144.4 20.4 %collective-permute-start.21 = (f32[2,4,1,128]{3,2,1,0:T(1,128)S(1)}, f32[2,4,1,128]{3,2,1,0:T(1,128)S(1)}, u32[]{:S(2)}, u32[]{:S(2)}) collective-permute-start(f32[2,4,1,128]{3,2,1,0:T(1,128)S(1)} %slice.645), channel_id=1, source_target_pairs={{0,4},{1,5},{2,6},{3,7},{8,12},{9,13},{10,14},{11,15},{16,20},{17,... | collective-permute-start | bytes 12296 | tf_op jit(solution)/shard_map/ppermute | solution.py:14
  147.4 17.3 %collective-permute-start.23 = (f32[2,1,16,128]{3,2,1,0:T(8,128)S(1)}, f32[2,1,16,128]{3,2,1,0:T(8,128)S(1)}, u32[]{:S(2)}, u32[]{:S(2)}) collective-permute-start(f32[2,1,16,128]{3,2,1,0:T(8,128)S(1)} %slice.806), channel_id=1, source_target_pairs={{0,8},{8,16},{16,24},{1,9},{9,17},{17,25},{2,10},{10,18},{18,26},{... | collective-permute-start | bytes 49160 | tf_op jit(solution)/shard_map/ppermute | solution.py:14
  151.7 13.0 %collective-permute-start.22 = (f32[2,4,16,1]{3,2,1,0:T(8,128)S(1)}, f32[2,4,16,1]{3,2,1,0:T(8,128)S(1)}, u32[]{:S(2)}, u32[]{:S(2)}) collective-permute-start(f32[2,4,16,1]{3,2,1,0:T(8,128)S(1)} %slice.800), channel_id=1, source_target_pairs={{0,1},{1,2},{2,3},{4,5},{5,6},{6,7},{8,9},{9,10},{10,11},{12,13},{... | collective-permute-start | bytes 1544 | tf_op jit(solution)/shard_map/ppermute | solution.py:14
  164.9 29.8 %copy-start.4 = (f32[3,4,16,128]{3,2,1,0:T(8,128)}, f32[3,4,16,128]{3,2,1,0:T(8,128)S(1)}, u32[]{:S(2)}) copy-start(f32[3,4,16,128]{3,2,1,0:T(8,128)S(1)} %fusion.14) | copy-start | bytes 294916
  184.3 9.3 %all-to-all-start = ((f32[8,3,192,1]{2,3,1,0:T(1,128)}), f32[8,3,192,1]{2,3,1,0:T(1,128)S(1)}, u32[]{:S(2)}, u32[]{:S(2)}) async-start(f32[8,3,192,1]{2,3,1,0:T(1,128)} %constant_dynamic-update-slice_fusion), calls=%async_computation | async-start | bytes 49152 | tf_op jit(solution)/shard_map/all_to_all | solution.py:126
